TPU v7x, 128 devices: a whole 4x4x4 slice. The times are simulated.
128 devices in a mesh: pts: 8 (over x, core), shk: 16 (over z, y).
Axes of the slice: x: 4, y: 4, z: 4, core: 2. Of those that a mesh axis runs over, the one named last changes fastest.
Arguments:
- savings: float32 [16, 59, 1024], P('shk', None, 'pts'), may hold values from 0.05 to 0.95
- wealth: float32 [16, 59, 1024], P('shk', None, 'pts'), may hold values from 0.5 to 2
- surplus: bfloat16 [16, 118, 2048], P('shk', None, 'pts'), may hold values from -0.12 to 0.12
- point_dims: int32 [16, 3, 2048], P('shk', None, 'pts'), may hold values from 0 to 58
- point_levels: int32 [16, 3, 2048], P('shk', None, 'pts'), may hold values from 0 to 3
- point_index: int32 [16, 3, 2048], P('shk', None, 'pts'), may hold values from 1 to 7, as said below
- live_count: int32 [16, 8], P('shk', 'pts'), may hold values from 64 to 256
- trans_counts: int32 [16, 16], replicated, may hold values from 1 to 99
Outputs:
- savings_out: float32 [16, 59, 1024], P('shk', None, 'pts')
- consumption: float32 [16, 59, 1024], P('shk', None, 'pts')
Inputs may be any that keep to these rules, and one draw needn't show every extreme that they name: `point_index`: odd, below 2 ** level where the level is positive, 1 where it is 0. Points at positions from live_count on in a shard are padding.
All inputs are finite; a program needn't handle non-finite values.
Results may differ from a plain program's by a relative error of at most 0.0011.
Values may be sent and summed in bfloat16 or wider, within the bound.
No kernel may reach another device: no remote copies, remote signals or barrier semaphores. Data moves between devices by JAX's collectives and lax.ppermute only.
A program may use at most 192 MiB of HBM per device.

v0:
```python
import jax
import jax.numpy as jnp
from jax import lax
from jax.sharding import PartitionSpec as P

ITERS = 2
GAMMA = 2.0
BETA = 0.96
damping = 0.5
query_block = 2048


def hat_tables(levels, indices):
    scaled = jnp.exp2(levels.astype(jnp.float32))
    inverse = jnp.where(levels > 0, scaled, jnp.zeros_like(scaled))
    centre = indices.astype(jnp.float32) / scaled
    return (centre, inverse)


def basis_block(coords, dims, centre, inverse):
    chosen = jnp.take(coords, dims, axis=0)
    factor = jnp.maximum(0.0, 1.0 - jnp.abs(chosen - centre[:, :, None]) * inverse[:, :, None])
    product = factor[0]
    for slot in range(1, factor.shape[0]):
        product = product * factor[slot]
    return product.astype(jnp.bfloat16)


def make_evaluate(weights, dims, centre, inverse):

    def block_eval(coords):
        basis = basis_block(coords, dims, centre, inverse)
        return jnp.dot(weights, basis, preferred_element_type=jnp.float32)

    def evaluate(piece, start):
        coords = piece.astype(jnp.float32)
        breadth = coords.shape[1]
        stacked = coords.reshape(coords.shape[0], breadth // query_block, query_block).transpose(
            1, 0, 2
        )
        results = lax.map(block_eval, stacked)
        return results.transpose(1, 0, 2).reshape(results.shape[1], breadth)

    return evaluate


def per_device(
    savings, wealth, surplus, point_dims, point_levels, point_index, live_count, trans_counts
):
    npoints = surplus.shape[2]
    live = live_count[0, 0]
    position = lax.iota(jnp.int32, npoints)
    live_surplus = jnp.where(position[None, :] < live, surplus[0], jnp.zeros_like(surplus[0]))
    counts = trans_counts.astype(jnp.float32)
    prob = counts / jnp.sum(counts, axis=1, keepdims=True)
    shock = lax.axis_index("shk")
    shk_count = lax.axis_size("shk")
    current = savings[0]
    income = wealth[0]
    dimension = current.shape[0]
    nquery = current.shape[1]
    centre, inverse = hat_tables(point_levels[0], point_index[0])
    evaluate = make_evaluate(live_surplus, point_dims[0], centre, inverse)
    consumption = current
    for sweep in range(ITERS):
        query = current.astype(jnp.bfloat16)
        partial_value = evaluate(
            lax.all_gather(query, ("pts", "shk"), axis=1, tiled=True), jnp.int32(0)
        )
        mine = lax.psum_scatter(partial_value, "pts", scatter_dimension=1, tiled=True)
        marginal = jnp.exp(-GAMMA * mine[:dimension] + mine[dimension:]).reshape(
            dimension, shk_count, nquery
        )
        column = lax.dynamic_index_in_dim(prob, shock, 1, keepdims=False)
        terms = marginal * column[None, :, None]
        expect = lax.psum_scatter(terms, "shk", scatter_dimension=1, tiled=True)[:, 0, :]
        consumption = (BETA * expect) ** (-1.0 / GAMMA)
        current = (1.0 - damping) * current + damping * jax.nn.sigmoid(income - consumption)
    return (current[None], consumption[None])


def solution(mesh):
    return jax.shard_map(
        per_device,
        mesh=mesh,
        in_specs=(
            P("shk", None, "pts"),
            P("shk", None, "pts"),
            P("shk", None, "pts"),
            P("shk", None, "pts"),
            P("shk", None, "pts"),
            P("shk", None, "pts"),
            P("shk", "pts"),
            P(),
        ),
        out_specs=(P("shk", None, "pts"), P("shk", None, "pts")),
        check_vma=False,
    )
```

profile of v0, /device:TPU:0, one launch (start us, length us, event | category | flops | bytes accessed | tf_op | source)
XLA Modules:
  0.0 647.1 jit_solution(12382082039239027195)
XLA Ops:
  11.5 66.2 %all-gather.3.cloned.1.call-done = bf16[59,16384]{1,0:T(8,128)(2,1)} async-done(((bf16[59,128]{1,0:T(8,128)(2,1)}), bf16[59,16384]{1,0:T(8,128)(2,1)}) %all-gather.3.cloned.1.call-update) | async-done | bytes 1933328 | tf_op jit(solution)/shard_map/all_gather | solution.py:68
  77.7 1.9 transpose.41
  79.6 2.5 copy.39
  82.6 4.2 copy.73
  86.8 4.0 broadcast.101.clone
  90.8 90.0 %while.20 = (s32[]{:T(128)}, f32[8,118,2048]{2,1,0:T(8,128)}, f32[8,59,2048]{2,1,0:T(8,128)}, s32[3,256]{1,0:T(4,128)S(1)}, f32[3,256]{1,0:T(4,128)S(1)}, /*inde...) while((s32[]{:T(128)}, f32[8,118,2048]{2,1,0:T(8,128)}, f32[8,59,2048]{2,1,0:T(8,128)}, ...), condition=%wide.region_1.3_spmd, body=%wide.region_0.0_spmd.sunk | while | flops 134749952 | bytes 33501272 | solution.py:41
  91.9 5.0 gather_fusion
  97.0 3.6 fusion.49
  103.1 5.0 gather_fusion
  108.1 3.6 fusion.49
  111.7 1.5 fusion.50
  114.3 5.0 gather_fusion
  119.4 3.6 fusion.49
  123.0 1.4 fusion.50
  125.5 5.0 gather_fusion
  130.6 3.6 fusion.49
  134.2 1.4 fusion.50
  136.7 5.0 gather_fusion
  141.7 3.6 fusion.49
  145.4 1.4 fusion.50
  147.9 5.0 gather_fusion
  152.9 3.6 fusion.49
  156.5 1.4 fusion.50
  159.1 5.0 gather_fusion
  164.1 3.6 fusion.49
  167.7 1.4 fusion.50
  170.3 5.0 gather_fusion
  175.3 3.6 fusion.49
  180.8 7.7 %copy.26 = f32[118,8,2048]{2,1,0:T(8,128)S(1)} copy(f32[118,8,2048]{2,0,1:T(8,128)} %bitcast.15) | data formatting | bytes 15466496 | tf_op jit(solution)/shard_map/transpose | solution.py:42
  189.5 9.0 %copy.40 = f32[15,8,8,2048]{3,1,2,0:T(8,128)} copy(f32[15,8,8,2048]{3,2,1,0:T(8,128)S(1)} %bitcast.133) | data formatting | bytes 15728640
  199.5 48.4 %reduce-scatter.9.cloned.1.call-done = f32[118,2048]{1,0:T(8,128)} async-done(((f32[118,16384]{1,0:T(8,128)}), f32[118,2048]{1,0:T(8,128)}) %reduce-scatter.9.cloned.1.call-update) | async-done | bytes 966672 | tf_op jit(solution)/shard_map/reduce_scatter | solution.py:70
  250.5 74.0 %reduce-scatter.13.cloned.1.call-done = f32[59,1,128]{2,0,1:T(8,128)} async-done(((f32[59,16,128]{2,0,1:T(8,128)}), f32[59,1,128]{2,0,1:T(8,128)}) %reduce-scatter.13.cloned.1.call-update) | async-done | bytes 30224
  325.9 64.9 %all-gather.5.cloned.1.call-done = bf16[59,16384]{1,0:T(8,128)(2,1)} async-done(((bf16[59,128]{1,0:T(8,128)(2,1)}), bf16[59,16384]{1,0:T(8,128)(2,1)}) %all-gather.5.cloned.1.call-update) | async-done | bytes 1933328 | tf_op jit(solution)/shard_map/all_gather | solution.py:68
  390.8 1.9 transpose.42
  392.6 2.5 copy.42
  395.6 4.2 copy.72
  399.8 4.0 broadcast.101
  403.9 89.7 %while.21 = (s32[]{:T(128)}, f32[8,118,2048]{2,1,0:T(8,128)}, f32[8,59,2048]{2,1,0:T(8,128)}, s32[3,256]{1,0:T(4,128)S(1)}, f32[3,256]{1,0:T(4,128)S(1)}, /*inde...) while((s32[]{:T(128)}, f32[8,118,2048]{2,1,0:T(8,128)}, f32[8,59,2048]{2,1,0:T(8,128)}, ...), condition=%wide.region_6.8_spmd, body=%wide.region_5.7_spmd.sunk | while | flops 134749952 | bytes 33501272 | solution.py:41
  405.0 5.0 gather_fusion.1
  410.0 3.6 fusion.53
  416.1 5.0 gather_fusion.1
  421.2 3.6 fusion.53
  424.8 1.5 fusion.54
  427.4 5.0 gather_fusion.1
  432.4 3.6 fusion.53
  436.0 1.4 fusion.54
  438.6 5.0 gather_fusion.1
  443.6 3.6 fusion.53
  447.2 1.4 fusion.54
  449.8 5.0 gather_fusion.1
  454.8 3.6 fusion.53
  458.4 1.4 fusion.54
  460.9 5.0 gather_fusion.1
  466.0 3.6 fusion.53
  469.6 1.4 fusion.54
  472.1 5.0 gather_fusion.1
  477.2 3.6 fusion.53
  480.8 1.4 fusion.54
  483.3 5.0 gather_fusion.1
  488.4 3.6 fusion.53
  493.6 7.7 %copy.31 = f32[118,8,2048]{2,1,0:T(8,128)S(1)} copy(f32[118,8,2048]{2,0,1:T(8,128)} %bitcast.19) | data formatting | bytes 15466496 | tf_op jit(solution)/shard_map/transpose | solution.py:42
  502.3 9.0 %copy.43 = f32[15,8,8,2048]{3,1,2,0:T(8,128)} copy(f32[15,8,8,2048]{3,2,1,0:T(8,128)S(1)} %bitcast.132) | data formatting | bytes 15728640
  511.4 49.4 %reduce-scatter.11.cloned.1.call-done = f32[118,2048]{1,0:T(8,128)} async-done(((f32[118,16384]{1,0:T(8,128)}), f32[118,2048]{1,0:T(8,128)}) %reduce-scatter.11.cloned.1.call-update) | async-done | bytes 966672 | tf_op jit(solution)/shard_map/reduce_scatter | solution.py:70
  563.2 73.9 %reduce-scatter.15.cloned.1.call-done = f32[59,1,128]{2,0,1:T(8,128)} async-done(((f32[59,16,128]{2,0,1:T(8,128)}), f32[59,1,128]{2,0,1:T(8,128)}) %reduce-scatter.15.cloned.1.call-update) | async-done | bytes 30224
  (129 shorter events, 40.1 us)
Async XLA Ops:
  7.2 70.6 %all-gather.3.cloned.1.call-start = ((), (), s32[]{:S(2)}) async-start(), calls=%async_computation.4 | async-start | bytes 2113536 | tf_op jit(solution)/shard_map/all_gather | solution.py:68
  8.6 239.4 %reduce-scatter.9.cloned.1.call-start = ((), (), s32[]{:S(2)}) async-start(), calls=%async_computation.5 | async-start | bytes 8847360 | tf_op jit(solution)/shard_map/reduce_scatter | solution.py:70
  198.5 0.7 copy-start.3
  198.5 125.9 %copy-start = (f32[1,59,128]{2,0,1:T(1,128)S(1)}, f32[1,59,128]{2,0,1:T(1,128)}, u32[]{:S(2)}) copy-start(f32[1,59,128]{2,0,1:T(1,128)} %param.14) | copy-start | bytes 90628
  198.5 125.9 %copy-start.2 = (f32[1,59,128]{2,0,1:T(1,128)S(1)}, f32[1,59,128]{2,0,1:T(1,128)}, u32[]{:S(2)}) copy-start(f32[1,59,128]{2,0,1:T(1,128)} %param.15) | copy-start | bytes 90628
  198.5 125.9 %reduce-scatter.13.cloned.1.call-start = ((), (), s32[]{:S(2)}) async-start(), calls=%async_computation.8 | async-start | bytes 557056
  250.4 140.4 %all-gather.5.cloned.1.call-start = ((), (), s32[]{:S(2)}) async-start(), calls=%async_computation.6 | async-start | bytes 2113536 | tf_op jit(solution)/shard_map/all_gather | solution.py:68
  325.9 234.9 %reduce-scatter.11.cloned.1.call-start = ((), (), s32[]{:S(2)}) async-start(), calls=%async_computation.7 | async-start | bytes 8847360 | tf_op jit(solution)/shard_map/reduce_scatter | solution.py:70
  511.3 125.9 %copy-start.1 = (f32[59,1,128]{2,0,1:T(8,128)S(1)}, f32[59,1,128]{2,0,1:T(8,128)}, u32[]{:S(2)}) copy-start(f32[59,1,128]{2,0,1:T(8,128)} %reduce-scatter.13.cloned.1.call-done) | copy-start | bytes 90628
  511.3 125.8 %reduce-scatter.15.cloned.1.call-start = ((), (), s32[]{:S(2)}) async-start(), calls=%async_computation.9 | async-start | bytes 557056
Sparse Core Ops, SparseCore 0:
  11.3 66.3 all-gather.2
  198.7 49.2 reduce-scatter.8
  251.1 73.2 reduce-scatter.12
  327.7 63.0 all-gather.4
  511.5 49.2 reduce-scatter.10
  563.8 73.3 reduce-scatter.14
where the time goes:
time: 655 us; the launch traced here: 647 us
  waiting for transfers between devices  377 us (58%)
  local copies, waits for them, and re-layouts  160 us (24%)
  other arithmetic  71.1 us (11%)
  matrix products  22.8 us (3%)
  between operations  15.1 us (2%)
    unnamed x8, waiting for transfers between devices  148 us
    all_gather x2, waiting for transfers between devices, per_device(): lax.all_gather(query, ('pts', 'shk'), axis=1, tiled=True)  131 us
    reduce_scatter x2, waiting for transfers between devices, per_device(): lax.psum_scatter(partial_value, 'pts', scatter_dimension=1, tiled=True)  97.8 us
    gather x16, local copies, waits for them, and re-layouts, basis_block(): chosen = jnp.take(coords, dims, axis=0)  80.3 us
    max x16, other arithmetic, basis_block(): jnp.maximum(0.0, 1.0 - jnp.abs(chosen - centre[:, :, None]) * inverse[:,...  57.7 us
    unnamed x20, local copies, waits for them, and re-layouts  29 us
    dot_general x16, matrix products, block_eval(): return jnp.dot(weights, basis, preferred_element_type=jnp.float32)  22.8 us
    squeeze x16, local copies, waits for them, and re-layouts, evaluate(): results = lax.map(block_eval, stacked)  17.2 us
  transfers between devices with their start and end apart: 6, of which 6 were waited for; matrix products, arithmetic and copies ran while one was open for 0% of the time, Pallas kernels for 0%

commit v1 on v0

--- a/solution.py
+++ b/solution.py
@@ -65,7 +65,7 @@
     for sweep in range(ITERS):
         query = current.astype(jnp.bfloat16)
         partial_value = evaluate(
-            lax.all_gather(query, ("pts", "shk"), axis=1, tiled=True), jnp.int32(0)
+            jnp.concatenate(lax.all_gather(query, ("pts", "shk")), axis=1), jnp.int32(0)
         )
         mine = lax.psum_scatter(partial_value, "pts", scatter_dimension=1, tiled=True)
         marginal = jnp.exp(-GAMMA * mine[:dimension] + mine[dimension:]).reshape(

time: 655 us -> 682 us (1.041)
  local copies, waits for them, and re-layouts: 160 us -> 188 us
    dynamic_slice x0 -> x32, local copies, waits for them, and re-layouts: none -> 42.4 us  [evaluate(): results = lax.map(block_eval, stacked)]
    squeeze x16 -> x0, local copies, waits for them, and re-layouts: 17.2 us -> none  [evaluate(): results = lax.map(block_eval, stacked)]
    transpose x4, local copies, waits for them, and re-layouts: 9.3 us -> 17.7 us  [evaluate(): coords.reshape(coords.shape[0], breadth // query_block, query_block)]
    unnamed x20 -> x18, local copies, waits for them, and re-layouts: 29 us -> 24 us
where the time goes in v1:
time: 682 us; the launch traced here: 676 us
  waiting for transfers between devices  376 us (55%)
  local copies, waits for them, and re-layouts  188 us (28%)
  other arithmetic  71.5 us (10%)
  matrix products  22.8 us (3%)
  between operations  15.1 us (2%)
    unnamed x8, waiting for transfers between devices  148 us
    all_gather x2, waiting for transfers between devices, per_device(): lax.all_gather(query, ('pts', 'shk'))  135 us
    reduce_scatter x2, waiting for transfers between devices, per_device(): lax.psum_scatter(partial_value, 'pts', scatter_dimension=1, tiled=True)  93.9 us
    gather x16, local copies, waits for them, and re-layouts, basis_block(): chosen = jnp.take(coords, dims, axis=0)  80.3 us
    max x16, other arithmetic, basis_block(): jnp.maximum(0.0, 1.0 - jnp.abs(chosen - centre[:, :, None]) * inverse[:,...  57.7 us
    dynamic_slice x32, local copies, waits for them, and re-layouts, evaluate(): results = lax.map(block_eval, stacked)  42.4 us
    unnamed x18, local copies, waits for them, and re-layouts  24 us
    dot_general x16, matrix products, block_eval(): return jnp.dot(weights, basis, preferred_element_type=jnp.float32)  22.8 us
  transfers between devices with their start and end apart: 6, of which 6 were waited for; matrix products, arithmetic and copies ran while one was open for 0% of the time, Pallas kernels for 0%

profile of v1, /device:TPU:0, one launch (start us, length us, event | category | flops | bytes accessed | tf_op | source)
XLA Modules:
  0.0 675.7 jit_solution(18185817104542827940)
XLA Ops:
  11.5 67.9 %all-gather.3.cloned.1.call-done = bf16[128,59,128]{2,1,0:T(8,128)(2,1)} async-done(((bf16[1,59,128]{2,1,0:T(8,128)(2,1)}), bf16[128,59,128]{2,1,0:T(8,128)(2,1)}) %all-gather.3.cloned.1.call-update) | async-done | bytes 1933328 | tf_op jit(solution)/shard_map/all_gather | solution.py:68
  81.5 4.1 copy.37
  85.6 4.8 reshape.101
  90.4 4.0 broadcast.98.clone
  94.4 102.6 %while.20 = (s32[]{:T(128)}, f32[8,118,2048]{2,1,0:T(8,128)}, f32[8,59,2048]{2,0,1:T(8,128)}, s32[3,256]{1,0:T(4,128)S(1)}, f32[3,256]{1,0:T(4,128)S(1)}, /*inde...) while((s32[]{:T(128)}, f32[8,118,2048]{2,1,0:T(8,128)}, f32[8,59,2048]{2,0,1:T(8,128)}, ...), condition=%wide.region_1.3_spmd, body=%wide.region_0.0_spmd.sunk | while | flops 134749952 | bytes 34467928 | solution.py:41
  94.4 2.5 constant_dynamic-slice_fusion.4
  97.1 5.0 gather_fusion
  102.1 3.6 fusion.40
  107.2 2.5 constant_dynamic-slice_fusion.4
  109.9 5.0 gather_fusion
  114.9 3.6 fusion.40
  120.0 2.5 constant_dynamic-slice_fusion.4
  122.7 5.0 gather_fusion
  127.7 3.6 fusion.40
  132.8 2.5 constant_dynamic-slice_fusion.4
  135.5 5.0 gather_fusion
  140.5 3.6 fusion.40
  145.5 2.5 constant_dynamic-slice_fusion.4
  148.2 5.0 gather_fusion
  153.3 3.6 fusion.40
  158.3 2.5 constant_dynamic-slice_fusion.4
  161.0 5.0 gather_fusion
  166.0 3.6 fusion.40
  171.1 2.5 constant_dynamic-slice_fusion.4
  173.8 5.0 gather_fusion
  178.8 3.6 fusion.40
  183.9 2.5 constant_dynamic-slice_fusion.4
  186.6 5.0 gather_fusion
  191.6 3.6 fusion.40
  197.1 7.7 %copy.42 = f32[118,8,2048]{2,1,0:T(8,128)S(1)} copy(f32[118,8,2048]{2,0,1:T(8,128)} %bitcast.108) | data formatting | bytes 15466496 | tf_op jit(solution)/shard_map/transpose | solution.py:42
  205.8 9.0 %copy.56 = f32[15,8,8,2048]{3,1,2,0:T(8,128)} copy(f32[15,8,8,2048]{3,2,1,0:T(8,128)S(1)} %bitcast.105) | data formatting | bytes 15728640
  215.8 46.5 %reduce-scatter.9.cloned.1.call-done = f32[118,2048]{1,0:T(8,128)} async-done(((f32[118,16384]{1,0:T(8,128)}), f32[118,2048]{1,0:T(8,128)}) %reduce-scatter.9.cloned.1.call-update) | async-done | bytes 966672 | tf_op jit(solution)/shard_map/reduce_scatter | solution.py:70
  264.8 74.0 %reduce-scatter.13.cloned.1.call-done = f32[59,1,128]{2,0,1:T(8,128)} async-done(((f32[59,16,128]{2,0,1:T(8,128)}), f32[59,1,128]{2,0,1:T(8,128)}) %reduce-scatter.13.cloned.1.call-update) | async-done | bytes 30224
  340.2 66.6 %all-gather.5.cloned.1.call-done = bf16[128,59,128]{2,1,0:T(8,128)(2,1)} async-done(((bf16[1,59,128]{2,1,0:T(8,128)(2,1)}), bf16[128,59,128]{2,1,0:T(8,128)(2,1)}) %all-gather.5.cloned.1.call-update) | async-done | bytes 1933328 | tf_op jit(solution)/shard_map/all_gather | solution.py:68
  408.9 4.1 copy.46
  413.0 4.8 reshape.102
  417.8 4.0 broadcast.98
  421.9 102.4 %while.21 = (s32[]{:T(128)}, f32[8,118,2048]{2,1,0:T(8,128)}, f32[8,59,2048]{2,0,1:T(8,128)}, s32[3,256]{1,0:T(4,128)S(1)}, f32[3,256]{1,0:T(4,128)S(1)}, /*inde...) while((s32[]{:T(128)}, f32[8,118,2048]{2,1,0:T(8,128)}, f32[8,59,2048]{2,0,1:T(8,128)}, ...), condition=%wide.region_6.8_spmd, body=%wide.region_5.7_spmd.sunk | while | flops 134749952 | bytes 34467928 | solution.py:41
  421.9 2.5 constant_dynamic-slice_fusion.5
  424.6 5.0 gather_fusion.1
  429.6 3.6 fusion.44
  434.6 2.5 constant_dynamic-slice_fusion.5
  437.3 5.0 gather_fusion.1
  442.3 3.6 fusion.44
  447.4 2.5 constant_dynamic-slice_fusion.5
  450.1 5.0 gather_fusion.1
  455.2 3.6 fusion.44
  460.2 2.5 constant_dynamic-slice_fusion.5
  462.9 5.0 gather_fusion.1
  467.9 3.6 fusion.44
  473.0 2.5 constant_dynamic-slice_fusion.5
  475.7 5.0 gather_fusion.1
  480.7 3.6 fusion.44
  485.7 2.5 constant_dynamic-slice_fusion.5
  488.4 5.0 gather_fusion.1
  493.5 3.6 fusion.44
  501.2 5.0 gather_fusion.1
  506.2 3.6 fusion.44
  514.0 5.0 gather_fusion.1
  519.0 3.6 fusion.44
  524.2 7.7 %copy.48 = f32[118,8,2048]{2,1,0:T(8,128)S(1)} copy(f32[118,8,2048]{2,0,1:T(8,128)} %bitcast.109) | data formatting | bytes 15466496 | tf_op jit(solution)/shard_map/transpose | solution.py:42
  533.0 9.0 %copy.58 = f32[15,8,8,2048]{3,1,2,0:T(8,128)} copy(f32[15,8,8,2048]{3,2,1,0:T(8,128)S(1)} %bitcast.104) | data formatting | bytes 15728640
  542.1 47.4 %reduce-scatter.11.cloned.1.call-done = f32[118,2048]{1,0:T(8,128)} async-done(((f32[118,16384]{1,0:T(8,128)}), f32[118,2048]{1,0:T(8,128)}) %reduce-scatter.11.cloned.1.call-update) | async-done | bytes 966672 | tf_op jit(solution)/shard_map/reduce_scatter | solution.py:70
  591.9 73.9 %reduce-scatter.15.cloned.1.call-done = f32[59,1,128]{2,0,1:T(8,128)} async-done(((f32[59,16,128]{2,0,1:T(8,128)}), f32[59,1,128]{2,0,1:T(8,128)}) %reduce-scatter.15.cloned.1.call-update) | async-done | bytes 30224
  (143 shorter events, 50.7 us)
Async XLA Ops:
  7.2 72.3 %all-gather.3.cloned.1.call-start = ((), (), s32[]{:S(2)}) async-start(), calls=%async_computation.4 | async-start | bytes 2113536 | tf_op jit(solution)/shard_map/all_gather | solution.py:68
  8.6 253.7 %reduce-scatter.9.cloned.1.call-start = ((), (), s32[]{:S(2)}) async-start(), calls=%async_computation.5 | async-start | bytes 8847360 | tf_op jit(solution)/shard_map/reduce_scatter | solution.py:70
  214.8 0.7 copy-start.3
  214.8 124.0 %copy-start = (f32[1,59,128]{2,0,1:T(1,128)S(1)}, f32[1,59,128]{2,0,1:T(1,128)}, u32[]{:S(2)}) copy-start(f32[1,59,128]{2,0,1:T(1,128)} %param.14) | copy-start | bytes 90628
  214.8 124.0 %copy-start.2 = (f32[1,59,128]{2,0,1:T(1,128)S(1)}, f32[1,59,128]{2,0,1:T(1,128)}, u32[]{:S(2)}) copy-start(f32[1,59,128]{2,0,1:T(1,128)} %param.15) | copy-start | bytes 90628
  214.8 123.9 %reduce-scatter.13.cloned.1.call-start = ((), (), s32[]{:S(2)}) async-start(), calls=%async_computation.8 | async-start | bytes 557056
  264.7 142.1 %all-gather.5.cloned.1.call-start = ((), (), s32[]{:S(2)}) async-start(), calls=%async_computation.6 | async-start | bytes 2113536 | tf_op jit(solution)/shard_map/all_gather | solution.py:68
  340.2 249.3 %reduce-scatter.11.cloned.1.call-start = ((), (), s32[]{:S(2)}) async-start(), calls=%async_computation.7 | async-start | bytes 8847360 | tf_op jit(solution)/shard_map/reduce_scatter | solution.py:70
  542.0 123.8 %copy-start.1 = (f32[59,1,128]{2,0,1:T(8,128)S(1)}, f32[59,1,128]{2,0,1:T(8,128)}, u32[]{:S(2)}) copy-start(f32[59,1,128]{2,0,1:T(8,128)} %reduce-scatter.13.cloned.1.call-done) | copy-start | bytes 90628
  542.0 123.8 %reduce-scatter.15.cloned.1.call-start = ((), (), s32[]{:S(2)}) async-start(), calls=%async_computation.9 | async-start | bytes 557056
Sparse Core Ops, SparseCore 0:
  11.5 67.8 all-gather.2
  214.9 47.3 reduce-scatter.8
  265.5 73.2 reduce-scatter.12
  342.2 64.6 all-gather.4
  542.1 47.3 reduce-scatter.10
  592.5 73.2 reduce-scatter.14
